TPU v7x, 256 devices: a whole 4x4x8 slice. The times are simulated.
256 devices in a mesh: row: 16 (over x_hi, y, core), col: 16 (over z, x_lo).
Axes of the slice: x: 4 (x_hi: 2, x_lo: 2; x = x_hi * 2 + x_lo), y: 4, z: 8, core: 2. Of those that a mesh axis runs over, the one named last changes fastest.
Arguments:
- vectors: float32 [96, 65536], P(None, ('col', 'row')), may hold values from -6 to 6
- blocks: float32 [16, 16, 176, 128, 128], P('row', 'col'), may hold values from -0.0546875 to 0.0546875
- block_row: int32 [16, 16, 176], P('row', 'col'), may hold values from 0 to 31
- block_col: int32 [16, 16, 176], P('row', 'col'), may hold values from 0 to 31
- block_count: int32 [16, 16], P('row', 'col'), may hold values from 22 to 176, as said below
- lower_bound: float32 [1], replicated, may hold values from -2.5 to -1.5
- upper_bound: float32 [1], replicated, may hold values from 1.5 to 2.5
Outputs:
- filtered: float32 [96, 65536], P(None, ('col', 'row'))
Inputs may be any that keep to these rules, and one draw needn't show every extreme that they name: `block_row`: local block row index within the device's band. `block_col`: local block column index within the device's band. `block_count`: in every row of the device grid one device has all 176 slots stored.
All inputs are finite; a program needn't handle non-finite values.
Results may differ from a plain program's by a relative error of at most 0.0003.
Values sent between devices are 32-bit elements; how exact they have to be, the bound alone decides.
No kernel may reach another device: no remote copies, remote signals or barrier semaphores. Data moves between devices by JAX's collectives and lax.ppermute only.
A program may use at most 128 MiB of HBM per device.

v0:
```python
import jax
import jax.numpy as jnp
from jax import lax
from jax.sharding import PartitionSpec as P

BS = 128


def spread(value, axis, source):
    kept = jnp.where(lax.axis_index(axis) == source, value, 0).astype(value.dtype)
    return lax.psum(kept, axis)


def local_products(col_tile, row_tile, device_blocks, rows_local, cols_local, live_mask):
    vector_count = col_tile.shape[0]
    col_blocks = col_tile.shape[1] // BS
    row_blocks = row_tile.shape[1] // BS
    col_view = col_tile.reshape(vector_count, col_blocks, BS)
    row_view = row_tile.reshape(vector_count, row_blocks, BS)
    source_col = jnp.take(col_view, cols_local, axis=1)
    forward = jnp.einsum("sij,vsj->vsi", device_blocks, source_col, precision=lax.Precision.HIGHEST)
    source_row = jnp.take(row_view, rows_local, axis=1)
    backward = jnp.einsum(
        "sij,vsi->vsj", device_blocks, source_row, precision=lax.Precision.HIGHEST
    )
    row_onehot = (jnp.arange(row_blocks)[:, None] == rows_local[None, :]).astype(
        jnp.float32
    ) * live_mask[None, :]
    col_onehot = (jnp.arange(col_blocks)[:, None] == cols_local[None, :]).astype(
        jnp.float32
    ) * live_mask[None, :]
    forward_part = jnp.einsum("rs,vsi->vri", row_onehot, forward, precision=lax.Precision.HIGHEST)
    backward_part = jnp.einsum("cs,vsj->vcj", col_onehot, backward, precision=lax.Precision.HIGHEST)
    return (forward_part.reshape(vector_count, -1), backward_part.reshape(vector_count, -1))


def apply_hamiltonian(vectors, device_blocks, rows_local, cols_local, live_mask):
    col_tile = lax.all_gather(vectors, "row", axis=1, tiled=True)
    row_index = lax.axis_index("row")
    col_index = lax.axis_index("col")
    col_count = lax.axis_size("col")
    row_ratio = lax.axis_size("row") // col_count
    piece_size = vectors.shape[1]
    owner_flag = (row_index // row_ratio == col_index).astype(jnp.float32)
    row_tile = spread(col_tile, "col", row_index // row_ratio)
    forward_part, backward_part = local_products(
        col_tile, row_tile, device_blocks, rows_local, cols_local, live_mask
    )
    row_total = lax.psum(forward_part, "col")
    placed = row_total * owner_flag
    column_total = lax.psum(placed, "row")
    backward_sum = lax.psum_scatter(backward_part, "row", scatter_dimension=1, tiled=True)
    return backward_sum + lax.dynamic_slice_in_dim(
        column_total, row_index * piece_size, piece_size, 1
    )


def body(vectors, blocks, block_row, block_col, block_count, lower_bound, upper_bound):
    device_blocks = blocks[0, 0]
    rows_local = block_row[0, 0]
    cols_local = block_col[0, 0]
    live_mask = (jnp.arange(device_blocks.shape[0]) < block_count[0, 0]).astype(jnp.float32)
    center = (upper_bound[0] + lower_bound[0]) / 2.0
    half_width = (upper_bound[0] - lower_bound[0]) / 2.0
    previous = vectors
    product = apply_hamiltonian(vectors, device_blocks, rows_local, cols_local, live_mask)
    current = (product - center * vectors) / half_width
    product = apply_hamiltonian(current, device_blocks, rows_local, cols_local, live_mask)
    following = 2.0 * (product - center * current) / half_width - previous
    previous, current = (current, following)
    return current


def solution(mesh):
    placed = (
        P(None, ("col", "row")),
        P("row", "col", None, None, None),
        P("row", "col", None),
        P("row", "col", None),
        P("row", "col"),
        P(),
        P(),
    )
    return jax.shard_map(
        body, mesh=mesh, in_specs=placed, out_specs=P(None, ("col", "row")), check_vma=False
    )
```

profile of v0, /device:TPU:32, one launch (start us, length us, event | category | flops | bytes accessed | tf_op | source)
XLA Modules:
  0.0 1001.6 jit_solution(16163257239828997144)
XLA Ops:
  9.3 52.8 %all-gather.3.cloned.1.call-done = f32[96,4096]{1,0:T(8,128)} async-done(((f32[96,256]{1,0:T(8,128)}), f32[96,4096]{1,0:T(8,128)}) %all-gather.3.cloned.1.call-update) | async-done | bytes 1572880 | tf_op jit(solution)/shard_map/all_gather | solution.py:38
  62.1 1.6 copy_bitcast_fusion.6
  63.7 4.5 gather_fusion.1
  68.2 26.9 %fusion.37 = f32[96,176,128]{2,0,1:T(8,128)S(1)} fusion(f32[1,1,176,128,128]{4,3,2,1,0:T(8,128)} %param.10, f32[176,96,128]{2,1,0:T(8,128)} %gather_fusion.1, pred[176]{0:T(512)(128)(4,1)S(1)} %compare_and_fusion.1), kind=kOutput, calls=%fused_computation.37 | convolution fusion | flops 3324051456 | bytes 28836016 | tf_op jit(solution)/shard_map/sij,vsj->vsi/dot_general | solution.py:21
  95.1 9.6 fusion.16
  104.7 2.3 copy.42
  107.0 1.4 copy_bitcast_fusion.7
  108.5 160.6 %all-reduce.13.cloned.1.call-done = (f32[96,32,128]{2,0,1:T(8,128)}, f32[96,4096]{1,0:T(8,128)}) async-done(((f32[96,32,128]{2,0,1:T(8,128)}, f32[96,4096]{1,0:T(8,128)}), (f32[96,32,128]{2,0,1:T(8,128)}, f32[96,4096]{1,0:T(8,128)})) %all-reduce.13.cloned.1.call-update) | async-done | bytes 3145744 | tf_op jit(solution)/shard_map/psum | solution.py:11
  269.1 2.8 broadcast_multiply_fusion.1
  272.0 4.5 gather_fusion
  276.5 14.7 %fusion.32 = f32[96,176,128]{2,0,1:T(8,128)S(1)} fusion(f32[1,1,176,128,128]{4,3,2,1,0:T(8,128)} %param.10, f32[176,96,128]{2,1,0:T(8,128)} %gather_fusion, pred[176]{0:T(512)(128)(4,1)S(1)} %compare_and_fusion), kind=kOutput, calls=%fused_computation.36 | convolution fusion | flops 3324051456 | bytes 28836016 | tf_op jit(solution)/shard_map/sij,vsi->vsj/dot_general | solution.py:23
  291.2 9.6 fusion.18
  300.8 2.3 copy.43
  304.4 115.3 %all-reduce.7.cloned.1.call-done = f32[96,4096]{1,0:T(8,128)} async-done(((f32[96,4096]{1,0:T(8,128)}), f32[96,4096]{1,0:T(8,128)}) %all-reduce.7.cloned.1.call-update) | async-done | bytes 1572880 | tf_op jit(solution)/shard_map/psum | solution.py:51
  419.8 81.7 %reduce-scatter.3.cloned.1.call-done = f32[96,256]{1,0:T(8,128)} async-done(((f32[96,4096]{1,0:T(8,128)}), f32[96,256]{1,0:T(8,128)}) %reduce-scatter.3.cloned.1.call-update) | async-done | bytes 98320 | tf_op jit(solution)/shard_map/reduce_scatter | solution.py:52
  501.5 1.6 subtract_divide_fusion
  503.2 49.5 %all-gather.5.cloned.1.call-done = f32[96,4096]{1,0:T(8,128)} async-done(((f32[96,256]{1,0:T(8,128)}), f32[96,4096]{1,0:T(8,128)}) %all-gather.5.cloned.1.call-update) | async-done | bytes 1572880 | tf_op jit(solution)/shard_map/all_gather | solution.py:38
  552.6 1.6 copy_bitcast_fusion.4
  554.2 4.5 gather_fusion.3
  558.7 26.9 %fusion.47 = f32[96,176,128]{2,0,1:T(8,128)S(1)} fusion(f32[1,1,176,128,128]{4,3,2,1,0:T(8,128)} %param.10, f32[176,96,128]{2,1,0:T(8,128)} %gather_fusion.3, pred[176]{0:T(512)(128)(4,1)S(1)} %compare_and_fusion.1), kind=kOutput, calls=%fused_computation.39 | convolution fusion | flops 3324051456 | bytes 28836016 | tf_op jit(solution)/shard_map/sij,vsj->vsi/dot_general | solution.py:21
  585.6 9.6 fusion.12
  595.2 2.3 copy.40
  597.4 1.4 copy_bitcast_fusion.5
  598.9 161.4 %all-reduce.11.cloned.1.call-done = (f32[96,32,128]{2,0,1:T(8,128)}, f32[96,4096]{1,0:T(8,128)}) async-done(((f32[96,32,128]{2,0,1:T(8,128)}, f32[96,4096]{1,0:T(8,128)}), (f32[96,32,128]{2,0,1:T(8,128)}, f32[96,4096]{1,0:T(8,128)})) %all-reduce.11.cloned.1.call-update) | async-done | bytes 3145744 | tf_op jit(solution)/shard_map/psum | solution.py:11
  760.4 2.8 broadcast_multiply_fusion
  763.5 4.5 gather_fusion.2
  767.9 14.3 %fusion.42 = f32[96,176,128]{2,0,1:T(8,128)S(1)} fusion(f32[1,1,176,128,128]{4,3,2,1,0:T(8,128)} %param.10, f32[176,96,128]{2,1,0:T(8,128)} %gather_fusion.2, pred[176]{0:T(512)(128)(4,1)S(1)} %compare_and_fusion), kind=kOutput, calls=%fused_computation.38 | convolution fusion | flops 3324051456 | bytes 28836016 | tf_op jit(solution)/shard_map/sij,vsi->vsj/dot_general | solution.py:23
  782.3 9.6 fusion.14
  791.8 2.3 copy.41
  794.1 116.9 %all-reduce.9.cloned.1.call-done = f32[96,4096]{1,0:T(8,128)} async-done(((f32[96,4096]{1,0:T(8,128)}), f32[96,4096]{1,0:T(8,128)}) %all-reduce.9.cloned.1.call-update) | async-done | bytes 1572880 | tf_op jit(solution)/shard_map/psum | solution.py:51
  911.1 81.9 %reduce-scatter.5.cloned.1.call-done = f32[96,256]{1,0:T(8,128)} async-done(((f32[96,4096]{1,0:T(8,128)}), f32[96,256]{1,0:T(8,128)}) %reduce-scatter.5.cloned.1.call-update) | async-done | bytes 98320 | tf_op jit(solution)/shard_map/reduce_scatter | solution.py:52
  992.9 1.6 divide_subtract_fusion
  (39 shorter events, 2.8 us)
Async XLA Ops:
  6.5 55.6 %all-gather.3.cloned.1.call-start = ((), (), s32[]{:S(2)}) async-start(), calls=%async_computation.2 | async-start | bytes 1671168 | tf_op jit(solution)/shard_map/all_gather | solution.py:38
  7.3 261.8 %all-reduce.13.cloned.1.call-start = ((), (), s32[]{:S(2)}) async-start(), calls=%async_computation.9 | async-start | bytes 6291456 | tf_op jit(solution)/shard_map/psum | solution.py:11
  68.2 26.9 %copy-start.6 = (s32[1,1,176]{2,1,0:T(1,128)S(1)}, s32[1,1,176]{2,1,0:T(1,128)}, u32[]{:S(2)}) copy-start(s32[1,1,176]{2,1,0:T(1,128)} %param.11) | copy-start | bytes 2116
  95.1 11.9 %copy-start.2 = (f32[96,4096]{1,0:T(8,128)S(1)}, f32[96,4096]{1,0:T(8,128)}, u32[]{:S(2)}) copy-start(f32[96,4096]{1,0:T(8,128)} %all-gather.3.cloned.1.call-done) | copy-start | bytes 4718596
  108.4 311.4 %all-reduce.7.cloned.1.call-start = ((), (), s32[]{:S(2)}) async-start(), calls=%async_computation.4 | async-start | bytes 3145728 | tf_op jit(solution)/shard_map/psum | solution.py:51
  269.1 2.9 copy-start
  271.9 229.6 %reduce-scatter.3.cloned.1.call-start = ((), (), s32[]{:S(2)}) async-start(), calls=%async_computation.3 | async-start | bytes 1671168 | tf_op jit(solution)/shard_map/reduce_scatter | solution.py:52
  276.5 14.7 %copy-start.7 = (s32[1,1,176]{2,1,0:T(1,128)S(1)}, s32[1,1,176]{2,1,0:T(1,128)}, u32[]{:S(2)}) copy-start(s32[1,1,176]{2,1,0:T(1,128)} %param.12) | copy-start | bytes 2116
  291.2 210.3 %copy-start.4 = (f32[96,256]{1,0:T(8,128)S(1)}, f32[96,256]{1,0:T(8,128)}, u32[]{:S(2)}) copy-start(f32[96,256]{1,0:T(8,128)} %param.9) | copy-start | bytes 294916
  303.1 249.6 %all-gather.5.cloned.1.call-start = ((), (), s32[]{:S(2)}) async-start(), calls=%async_computation.5 | async-start | bytes 1671168 | tf_op jit(solution)/shard_map/all_gather | solution.py:38
  503.1 257.2 %all-reduce.11.cloned.1.call-start = ((), (), s32[]{:S(2)}) async-start(), calls=%async_computation.8 | async-start | bytes 6291456 | tf_op jit(solution)/shard_map/psum | solution.py:11
  585.6 11.8 %copy-start.3 = (f32[96,4096]{1,0:T(8,128)S(1)}, f32[96,4096]{1,0:T(8,128)}, u32[]{:S(2)}) copy-start(f32[96,4096]{1,0:T(8,128)} %all-gather.5.cloned.1.call-done) | copy-start | bytes 4718596
  598.9 312.2 %all-reduce.9.cloned.1.call-start = ((), (), s32[]{:S(2)}) async-start(), calls=%async_computation.7 | async-start | bytes 3145728 | tf_op jit(solution)/shard_map/psum | solution.py:51
  760.4 3.1 copy-start.1
  763.2 229.7 %reduce-scatter.5.cloned.1.call-start = ((), (), s32[]{:S(2)}) async-start(), calls=%async_computation.6 | async-start | bytes 1671168 | tf_op jit(solution)/shard_map/reduce_scatter | solution.py:52
  782.3 210.7 %copy-start.5 = (f32[96,256]{1,0:T(8,128)S(1)}, f32[96,256]{1,0:T(8,128)}, u32[]{:S(2)}) copy-start(f32[96,256]{1,0:T(8,128)} %subtract_divide_fusion) | copy-start | bytes 294916
Sparse Core Ops, SparseCore 0:
  9.9 52.1 all-gather.2
  108.5 160.5 all-reduce.12
  272.0 147.6 all-reduce.6
  423.8 77.6 reduce-scatter.2
  503.9 48.6 all-gather.4
  599.0 161.3 all-reduce.10
  763.3 147.6 all-reduce.8
  915.3 77.6 reduce-scatter.4
where the time goes:
time: 1010 us; the launch traced here: 1000 us
  waiting for transfers between devices  821 us (81%)
  matrix products  121 us (12%)
  local copies, waits for them, and re-layouts  30.1 us (3%)
  between operations  15.9 us (2%)
  other arithmetic  13 us (1%)
    psum x2, waiting for transfers between devices, spread(): return lax.psum(kept, axis)  322 us
    psum x2, waiting for transfers between devices, apply_hamiltonian(): column_total = lax.psum(placed, 'row')  232 us
    reduce_scatter x2, waiting for transfers between devices, apply_hamiltonian(): lax.psum_scatter(backward_part, 'row', scatter_dimension=1, tiled=True)  164 us
    all_gather x2, waiting for transfers between devices, apply_hamiltonian(): col_tile = lax.all_gather(vectors, 'row', axis=1, tiled=True)  102 us
    dot_general x2, matrix products, local_products(): jnp.einsum('sij,vsj->vsi', device_blocks, source_col, precision=lax.Preci...  53.8 us
    dot_general x2, matrix products, local_products(): jnp.einsum('sij,vsi->vsj', device_blocks, source_row, precision=lax.Preci...  29 us
  transfers between devices with their start and end apart: 8, of which 8 were waited for; matrix products, arithmetic and copies ran while one was open for 6% of the time, Pallas kernels for 0%

commit v1 on v0

--- a/solution.py
+++ b/solution.py
@@ -35,7 +35,9 @@
 
 
 def apply_hamiltonian(vectors, device_blocks, rows_local, cols_local, live_mask):
-    col_tile = lax.all_gather(vectors, "row", axis=1, tiled=True)
+    col_tile = jnp.concatenate(
+        lax.all_to_all(jnp.stack([vectors] * lax.axis_size("row")), "row", 0, 0), axis=1
+    )
     row_index = lax.axis_index("row")
     col_index = lax.axis_index("col")
     col_count = lax.axis_size("col")

time: 1010 us -> 978 us (0.968)
  waiting for transfers between devices: 821 us -> 738 us
  blocking collectives: 0 us -> 28.2 us
  local copies, waits for them, and re-layouts: 30.1 us -> 49.6 us
    all_gather x2 -> x0, waiting for transfers between devices: 102 us -> none  [apply_hamiltonian(): col_tile = lax.all_gather(vectors, 'row', axis=1, tiled=True)]
    all_to_all x0 -> x1, blocking collectives: none -> 28.2 us  [apply_hamiltonian(): lax.all_to_all(jnp.stack([vectors] * lax.axis_size('row')), 'row', 0, 0)]
    all_to_all x0 -> x1, waiting for transfers between devices: none -> 21.6 us  [apply_hamiltonian(): lax.all_to_all(jnp.stack([vectors] * lax.axis_size('row')), 'row', 0, 0)]
  transfers between devices with their start and end apart: 8 -> 7, of which waited for: 8 -> 7; matrix products, arithmetic and copies ran while one was open for 6% -> 6% of each run, Pallas kernels for 0% -> 0%
where the time goes in v1:
time: 978 us; the launch traced here: 970 us
  waiting for transfers between devices  738 us (75%)
  matrix products  122 us (12%)
  local copies, waits for them, and re-layouts  49.6 us (5%)
  blocking collectives  28.2 us (3%)
  between operations  15.8 us (2%)
  other arithmetic  9.88 us (1%)
    psum x2, waiting for transfers between devices, spread(): return lax.psum(kept, axis)  320 us
    psum x2, waiting for transfers between devices, apply_hamiltonian(): column_total = lax.psum(placed, 'row')  233 us
    reduce_scatter x2, waiting for transfers between devices, apply_hamiltonian(): lax.psum_scatter(backward_part, 'row', scatter_dimension=1, tiled=True)  164 us
    dot_general x2, matrix products, local_products(): jnp.einsum('sij,vsj->vsi', device_blocks, source_col, precision=lax.Preci...  54.3 us
    dot_general x2, matrix products, local_products(): jnp.einsum('sij,vsi->vsj', device_blocks, source_row, precision=lax.Preci...  28.9 us
    all_to_all x1, blocking collectives, apply_hamiltonian(): lax.all_to_all(jnp.stack([vectors] * lax.axis_size('row')), 'row', 0, 0)  28.2 us
    all_to_all x1, waiting for transfers between devices, apply_hamiltonian(): lax.all_to_all(jnp.stack([vectors] * lax.axis_size('row')), 'row', 0, 0)  21.6 us
  transfers between devices with their start and end apart: 7, of which 7 were waited for; matrix products, arithmetic and copies ran while one was open for 6% of the time, Pallas kernels for 0%

profile of v1, /device:TPU:32, one launch (start us, length us, event | category | flops | bytes accessed | tf_op | source)
XLA Modules:
  0.0 970.4 jit_solution(8747368352828512050)
XLA Ops:
  6.5 2.2 stack.4
  8.7 7.0 all-to-all-start
  17.9 21.6 %all-to-all-done = f32[16,96,256]{2,1,0:T(8,128)S(1)} async-done(((f32[16,96,256]{2,1,0:T(8,128)}), f32[16,96,256]{2,1,0:T(8,128)S(1)}, u32[]{:S(2)}, u32[]{:S(2)}) %all-to-all-start) | async-done | bytes 1572896 | tf_op jit(solution)/shard_map/all_to_all | solution.py:39
  41.6 2.3 copy.20
  46.2 3.5 copy.17
  49.8 4.5 gather_fusion.1
  54.2 27.2 %fusion.37 = f32[96,176,128]{2,0,1:T(8,128)S(1)} fusion(f32[1,1,176,128,128]{4,3,2,1,0:T(8,128)} %param.10, f32[176,96,128]{2,1,0:T(8,128)} %gather_fusion.1, pred[176]{0:T(512)(128)(4,1)S(1)} %compare_and_fusion.1), kind=kOutput, calls=%fused_computation.37 | convolution fusion | flops 3324051456 | bytes 28836016 | tf_op jit(solution)/shard_map/sij,vsj->vsi/dot_general | solution.py:21
  81.5 9.6 fusion.16
  91.0 2.2 copy.46
  93.4 161.0 %all-reduce.13.cloned.1.call-done = (f32[96,32,128]{2,0,1:T(8,128)}, f32[96,4096]{1,0:T(8,128)}) async-done(((f32[96,32,128]{2,0,1:T(8,128)}, f32[96,4096]{1,0:T(8,128)}), (f32[96,32,128]{2,0,1:T(8,128)}, f32[96,4096]{1,0:T(8,128)})) %all-reduce.13.cloned.1.call-update) | async-done | bytes 3145744 | tf_op jit(solution)/shard_map/psum | solution.py:11
  254.4 2.8 broadcast_multiply_fusion.1
  257.3 4.5 gather_fusion
  261.8 14.5 %fusion.32 = f32[96,176,128]{2,0,1:T(8,128)S(1)} fusion(f32[1,1,176,128,128]{4,3,2,1,0:T(8,128)} %param.10, f32[176,96,128]{2,1,0:T(8,128)} %gather_fusion, pred[176]{0:T(512)(128)(4,1)S(1)} %compare_and_fusion), kind=kOutput, calls=%fused_computation.36 | convolution fusion | flops 3324051456 | bytes 28836016 | tf_op jit(solution)/shard_map/sij,vsi->vsj/dot_general | solution.py:23
  276.3 9.6 fusion.18
  285.8 2.3 copy.47
  289.5 115.6 %all-reduce.7.cloned.1.call-done = f32[96,4096]{1,0:T(8,128)} async-done(((f32[96,4096]{1,0:T(8,128)}), f32[96,4096]{1,0:T(8,128)}) %all-reduce.7.cloned.1.call-update) | async-done | bytes 1572880 | tf_op jit(solution)/shard_map/psum | solution.py:53
  405.1 81.9 %reduce-scatter.3.cloned.1.call-done = f32[96,256]{1,0:T(8,128)} async-done(((f32[96,4096]{1,0:T(8,128)}), f32[96,256]{1,0:T(8,128)}) %reduce-scatter.3.cloned.1.call-update) | async-done | bytes 98320 | tf_op jit(solution)/shard_map/reduce_scatter | solution.py:54
  488.1 28.2 %all_to_all.10 = f32[16,96,256]{2,1,0:T(8,128)S(1)} all-to-all(f32[16,96,256]{2,1,0:T(8,128)S(1)} %stack.5), channel_id=1, replica_groups=mesh['row'=16,'col'=16] {'row'}, dimensions={0} | all-to-all | bytes 3145728 | tf_op jit(solution)/shard_map/all_to_all | solution.py:39
  518.6 3.5 copy.23
  524.3 2.3 copy.26
  526.6 4.5 gather_fusion.3
  531.1 27.1 %fusion.47 = f32[96,176,128]{2,0,1:T(8,128)S(1)} fusion(f32[1,1,176,128,128]{4,3,2,1,0:T(8,128)} %param.10, f32[176,96,128]{2,1,0:T(8,128)} %gather_fusion.3, pred[176]{0:T(512)(128)(4,1)S(1)} %compare_and_fusion.1), kind=kOutput, calls=%fused_computation.39 | convolution fusion | flops 3324051456 | bytes 28836016 | tf_op jit(solution)/shard_map/sij,vsj->vsi/dot_general | solution.py:21
  558.2 9.6 fusion.12
  567.8 2.2 copy.44
  570.1 159.2 %all-reduce.11.cloned.1.call-done = (f32[96,32,128]{2,0,1:T(8,128)}, f32[96,4096]{1,0:T(8,128)}) async-done(((f32[96,32,128]{2,0,1:T(8,128)}, f32[96,4096]{1,0:T(8,128)}), (f32[96,32,128]{2,0,1:T(8,128)}, f32[96,4096]{1,0:T(8,128)})) %all-reduce.11.cloned.1.call-update) | async-done | bytes 3145744 | tf_op jit(solution)/shard_map/psum | solution.py:11
  729.3 2.8 broadcast_multiply_fusion
  732.2 4.5 gather_fusion.2
  736.7 14.5 %fusion.42 = f32[96,176,128]{2,0,1:T(8,128)S(1)} fusion(f32[1,1,176,128,128]{4,3,2,1,0:T(8,128)} %param.10, f32[176,96,128]{2,1,0:T(8,128)} %gather_fusion.2, pred[176]{0:T(512)(128)(4,1)S(1)} %compare_and_fusion), kind=kOutput, calls=%fused_computation.38 | convolution fusion | flops 3324051456 | bytes 28836016 | tf_op jit(solution)/shard_map/sij,vsi->vsj/dot_general | solution.py:23
  751.1 9.6 fusion.14
  760.7 2.3 copy.45
  763.0 117.0 %all-reduce.9.cloned.1.call-done = f32[96,4096]{1,0:T(8,128)} async-done(((f32[96,4096]{1,0:T(8,128)}), f32[96,4096]{1,0:T(8,128)}) %all-reduce.9.cloned.1.call-update) | async-done | bytes 1572880 | tf_op jit(solution)/shard_map/psum | solution.py:53
  880.0 81.7 %reduce-scatter.5.cloned.1.call-done = f32[96,256]{1,0:T(8,128)} async-done(((f32[96,4096]{1,0:T(8,128)}), f32[96,256]{1,0:T(8,128)}) %reduce-scatter.5.cloned.1.call-update) | async-done | bytes 98320 | tf_op jit(solution)/shard_map/reduce_scatter | solution.py:54
  (42 shorter events, 13.4 us)
Async XLA Ops:
  8.7 30.7 %all-to-all-start = ((f32[16,96,256]{2,1,0:T(8,128)}), f32[16,96,256]{2,1,0:T(8,128)S(1)}, u32[]{:S(2)}, u32[]{:S(2)}) async-start(f32[16,96,256]{2,1,0:T(8,128)} %stack.4), calls=%async_computation | async-start | bytes 3145728 | tf_op jit(solution)/shard_map/all_to_all | solution.py:39
  15.8 238.6 %all-reduce.13.cloned.1.call-start = ((), (), s32[]{:S(2)}) async-start(), calls=%async_computation.9 | async-start | bytes 6291456 | tf_op jit(solution)/shard_map/psum | solution.py:11
  54.2 27.2 %copy-start.3 = (s32[1,1,176]{2,1,0:T(1,128)S(1)}, s32[1,1,176]{2,1,0:T(1,128)}, u32[]{:S(2)}) copy-start(s32[1,1,176]{2,1,0:T(1,128)} %param.11) | copy-start | bytes 2116
  93.3 311.8 %all-reduce.7.cloned.1.call-start = ((), (), s32[]{:S(2)}) async-start(), calls=%async_computation.5 | async-start | bytes 3145728 | tf_op jit(solution)/shard_map/psum | solution.py:53
  254.4 2.9 copy-start
  257.2 229.8 %reduce-scatter.3.cloned.1.call-start = ((), (), s32[]{:S(2)}) async-start(), calls=%async_computation.4 | async-start | bytes 1671168 | tf_op jit(solution)/shard_map/reduce_scatter | solution.py:54
  261.8 14.5 %copy-start.4 = (s32[1,1,176]{2,1,0:T(1,128)S(1)}, s32[1,1,176]{2,1,0:T(1,128)}, u32[]{:S(2)}) copy-start(s32[1,1,176]{2,1,0:T(1,128)} %param.12) | copy-start | bytes 2116
  276.2 210.7 %copy-start.2 = (f32[96,256]{1,0:T(8,128)S(1)}, f32[96,256]{1,0:T(8,128)}, u32[]{:S(2)}) copy-start(f32[96,256]{1,0:T(8,128)} %param.9) | copy-start | bytes 294916
  288.1 441.2 %all-reduce.11.cloned.1.call-start = ((), (), s32[]{:S(2)}) async-start(), calls=%async_computation.8 | async-start | bytes 6291456 | tf_op jit(solution)/shard_map/psum | solution.py:11
  570.1 309.9 %all-reduce.9.cloned.1.call-start = ((), (), s32[]{:S(2)}) async-start(), calls=%async_computation.7 | async-start | bytes 3145728 | tf_op jit(solution)/shard_map/psum | solution.py:53
  729.3 2.9 copy-start.1
  732.2 229.6 %reduce-scatter.5.cloned.1.call-start = ((), (), s32[]{:S(2)}) async-start(), calls=%async_computation.6 | async-start | bytes 1671168 | tf_op jit(solution)/shard_map/reduce_scatter | solution.py:54
Sparse Core Ops, SparseCore 0:
  93.4 160.9 all-reduce.12
  257.3 147.7 all-reduce.6
  409.3 77.6 reduce-scatter.2
  570.2 159.0 all-reduce.10
  732.3 147.6 all-reduce.8
  884.1 77.6 reduce-scatter.4
